TPU v7x, 128 devices: a whole 4x4x4 slice. The times are simulated.
128 devices in a mesh: row: 32 (over x_hi, z, y), ch: 4 (over x_lo, core).
Axes of the slice: x: 4 (x_hi: 2, x_lo: 2; x = x_hi * 2 + x_lo), y: 4, z: 4, core: 2. Of those that a mesh axis runs over, the one named last changes fastest.
Arguments:
- pair_rep: float32 [256, 256, 128], P(('row', 'ch')), may hold values from -6 to 6
- pair_mask: int32 [256, 256], P(('row', 'ch')), may hold values from 0 to 1, as said below
- ln_in_gain: float32 [128], replicated, may hold values from 0.5 to 1.5
- ln_in_bias: float32 [128], replicated, may hold values from -3 to 3
- w_in: float32 [128, 640], replicated, may hold values from -0.5 to 0.5
- b_in: float32 [640], replicated, may hold values from -3 to 3
- ln_out_gain: float32 [128], replicated, may hold values from 0.5 to 1.5
- ln_out_bias: float32 [128], replicated, may hold values from -3 to 3
- w_out: float32 [128, 128], replicated, may hold values from -0.5 to 0.5
- b_out: float32 [128], replicated, may hold values from -3 to 3
- cotangent: float32 [256, 256, 128], P(('row', 'ch')), may hold values from -6 to 6
Outputs:
- update: float32 [256, 256, 128], P(('row', 'ch'))
- grad_pair: float32 [256, 256, 128], P(('row', 'ch'))
- grad_w_in: float32 [128, 640], replicated
- grad_w_out: float32 [128, 128], replicated
Inputs may be any that keep to these rules, and one draw needn't show every extreme that they name: pair_mask[i, k] = m_i m_k, where m is 1 for the residues present in the crop and 0 otherwise.
All inputs are finite; a program needn't handle non-finite values.
Results may differ from a plain program's by a relative error of at most 0.00009.
Values sent between devices are 32-bit elements; how exact they have to be, the bound alone decides.
No kernel may reach another device: no remote copies, remote signals or barrier semaphores. Data moves between devices by JAX's collectives and lax.ppermute only.
A program may use at most 64 MiB of HBM per device.

v0:
```python
import jax
import jax.numpy as jnp
from jax import lax
from jax.sharding import PartitionSpec as P

epsilon = 1e-05


def side_by_side(arrays, axis, split_dim, concat_dim, along):
    ends, at = ([], 0)
    for a in arrays[:-1]:
        at += a.shape[along]
        ends.append(at)
    both = jnp.concatenate(arrays, axis=along)
    return tuple(
        jnp.split(
            lax.all_to_all(both, axis, split_axis=split_dim, concat_axis=concat_dim, tiled=True),
            ends,
            axis=along,
        )
    )


def prelude(field, keep_mask, norm_gain, norm_bias, weights, offsets):
    channels = field.shape[-1]
    hidden = (weights.shape[1] - channels) // 4
    center = jnp.mean(field, -1, keepdims=True)
    spread = jnp.mean((field - center) ** 2, -1, keepdims=True)
    normed = (field - center) * lax.rsqrt(spread + epsilon) * norm_gain + norm_bias
    pieces = jnp.einsum(
        "ikc,cf->fik", normed, weights[:, : 4 * hidden], precision=lax.Precision.HIGHEST
    )
    pieces = pieces + offsets[: 4 * hidden, None, None]
    gate = jax.nn.sigmoid(
        jnp.einsum("ikc,cf->ikf", normed, weights[:, 4 * hidden :], precision=lax.Precision.HIGHEST)
        + offsets[4 * hidden :]
    )
    keep = keep_mask.astype(field.dtype)[None]
    left = keep * jax.nn.sigmoid(pieces[:hidden]) * pieces[hidden : 2 * hidden]
    right = keep * jax.nn.sigmoid(pieces[2 * hidden : 3 * hidden]) * pieces[3 * hidden :]
    return (left, right, gate)


def epilogue(product, gate, norm_gain, norm_bias, weights, offset):
    center = jnp.mean(product, 0, keepdims=True)
    spread = jnp.mean((product - center) ** 2, 0, keepdims=True)
    normed = (product - center) * lax.rsqrt(spread + epsilon) * norm_gain[
        :, None, None
    ] + norm_bias[:, None, None]
    projected = jnp.einsum("hij,hc->ijc", normed, weights, precision=lax.Precision.HIGHEST) + offset
    return gate * projected


def on_device(
    pair_rep,
    pair_mask,
    ln_in_gain,
    ln_in_bias,
    w_in,
    b_in,
    ln_out_gain,
    ln_out_bias,
    w_out,
    b_out,
    cotangent,
):
    row_count = pair_rep.shape[0]
    length = pair_rep.shape[1]
    hidden = w_out.shape[0]
    per_device = hidden // (lax.axis_size("row") * lax.axis_size("ch"))

    def local_prelude(field, weights):
        return prelude(field, pair_mask, ln_in_gain, ln_in_bias, weights, b_in)

    (left_rows, right_rows, gate), prelude_back = jax.vjp(local_prelude, pair_rep, w_in)
    row_shape = (hidden, 1, row_count, length)
    left_cols, right_cols = side_by_side(
        (left_rows.reshape(row_shape), right_rows.reshape(row_shape)), ("row", "ch"), 0, 2, 1
    )
    left_cols = left_cols.reshape(per_device, length, length)
    right_cols = right_cols.reshape(per_device, length, length)
    product = jnp.einsum("hik,hjk->hij", left_cols, right_cols, precision=lax.Precision.HIGHEST)
    product_rows = lax.all_to_all(
        product.reshape(per_device, 1, length, length),
        ("row", "ch"),
        split_axis=2,
        concat_axis=0,
        tiled=True,
    )
    product_rows = product_rows.reshape(hidden, row_count, length)

    def local_epilogue(prod_part, gate_part, weights):
        return epilogue(prod_part, gate_part, ln_out_gain, ln_out_bias, weights, b_out)

    update, epilogue_back = jax.vjp(local_epilogue, product_rows, gate, w_out)
    d_product, d_gate, d_wout = epilogue_back(cotangent)
    d_cols = lax.all_to_all(
        d_product.reshape(row_shape), ("row", "ch"), split_axis=0, concat_axis=2, tiled=True
    )
    d_cols = d_cols.reshape(per_device, length, length)
    d_left = jnp.einsum("hij,hjk->hik", d_cols, right_cols, precision=lax.Precision.HIGHEST)
    d_right = jnp.einsum("hij,hik->hjk", d_cols, left_cols, precision=lax.Precision.HIGHEST)
    col_shape = (per_device, 1, length, length)
    d_left, d_right = side_by_side(
        (d_left.reshape(col_shape), d_right.reshape(col_shape)), ("row", "ch"), 2, 0, 1
    )
    d_left = d_left.reshape(hidden, row_count, length)
    d_right = d_right.reshape(hidden, row_count, length)
    grad_pair, d_win = prelude_back((d_left, d_right, d_gate))
    wide = w_in.shape[1]
    terms = jnp.concatenate([d_win, d_wout], axis=1)
    terms = lax.all_to_all(terms, ("row", "ch"), split_axis=0, concat_axis=0, tiled=True)
    mine = jnp.sum(terms, 0, keepdims=True) / length
    whole = lax.all_to_all(
        jnp.broadcast_to(mine, terms.shape), ("row", "ch"), split_axis=0, concat_axis=0, tiled=True
    )
    return (update, grad_pair, whole[:, :wide], whole[:, wide:])


def solution(mesh):
    placed = (
        P(("row", "ch"), None, None),
        P(("row", "ch"), None),
        P(),
        P(),
        P(),
        P(),
        P(),
        P(),
        P(),
        P(),
        P(("row", "ch"), None, None),
    )
    return jax.shard_map(
        on_device,
        mesh=mesh,
        in_specs=placed,
        out_specs=(P(("row", "ch"), None, None), P(("row", "ch"), None, None), P(), P()),
        check_vma=False,
    )
```

profile of v0, /device:TPU:1, one launch (start us, length us, event | category | flops | bytes accessed | tf_op | source)
XLA Modules:
  0.0 128.7 jit_solution(5223931275819464922)
XLA Ops:
  1.4 1.1 copy.61
  3.5 1.1 fusion
  5.1 24.7 %all_to_all.72 = f32[128,2,2,256]{3,2,1,0:T(2,128)S(1)} all-to-all(f32[128,2,2,256]{3,2,1,0:T(2,128)S(1)} %copy.64), channel_id=1, replica_groups=mesh['row'=32,'ch'=4] {'row','ch'}, dimensions={0} | all-to-all | bytes 1048576 | tf_op jit(solution)/shard_map/all_to_all | solution.py:17
  31.0 1.0 copy.66
  31.9 4.9 %all-to-all-start.1 = ((f32[1,1,256,256]{3,1,0,2:T(1,128)}), f32[1,1,256,256]{3,1,0,2:T(1,128)S(1)}, u32[]{:S(2)}, u32[]{:S(2)}) async-start(f32[1,1,256,256]{3,1,0,2:T(1,128)} %copy.66), calls=%async_computation.1 | async-start | bytes 524288 | tf_op jit(solution)/shard_map/all_to_all | solution.py:83
  37.5 10.3 %all-to-all-done.1 = f32[1,1,256,256]{3,1,0,2:T(1,128)S(1)} async-done(((f32[1,1,256,256]{3,1,0,2:T(1,128)}), f32[1,1,256,256]{3,1,0,2:T(1,128)S(1)}, u32[]{:S(2)}, u32[]{:S(2)}) %all-to-all-start.1) | async-done | bytes 262176 | tf_op jit(solution)/shard_map/all_to_all | solution.py:83
  48.8 0.8 copy-done.1
  50.3 15.3 %all_to_all.73 = f32[128,1,2,256]{3,2,1,0:T(2,128)S(1)} all-to-all(f32[128,1,2,256]{3,2,1,0:T(2,128)S(1)} %copy.69), channel_id=1, replica_groups=mesh['row'=32,'ch'=4] {'row','ch'}, dimensions={0} | all-to-all | bytes 524288 | tf_op jit(solution)/shard_map/all_to_all | solution.py:97
  66.9 1.2 copy.70
  68.1 4.5 %all-to-all-start.3 = ((f32[1,2,256,256]{3,1,0,2:T(2,128)}), f32[1,2,256,256]{3,1,0,2:T(2,128)S(1)}, u32[]{:S(2)}, u32[]{:S(2)}) async-start(f32[1,2,256,256]{3,1,0,2:T(2,128)} %copy.70), calls=%async_computation.3 | async-start | bytes 1048576 | tf_op jit(solution)/shard_map/all_to_all | solution.py:17
  72.6 1.3 convolution_bitcast_fusion.4
  73.9 1.4 %fusion.52 = (f32[2,256,128]{2,1,0:T(8,128)}, f32[2,256,128]{2,1,0:T(8,128)S(1)}) fusion(f32[2,256,128]{2,1,0:T(8,128)S(1)} %fusion.6, f32[128]{0:T(128)S(1)} %copy-done.13, f32[128,128]{1,0:T(8,128)S(1)} %copy-done, f32[128]{0:T(128)S(1)} %copy-done.12, f32[128]{0:T(128)S(1)} %copy-done.9, f32[2,256]{1,0:T(2,128)S(1)} %get-tuple-element.33, ...), kind=kOutput, calls=%fused_computation.98 | convolution fusion | flops 101056512 | bytes 1119744 | tf_op jit(solution)/shard_map/jvp(hij,hc->ijc)/dot_general | solution.py:50
  75.9 10.1 %all-to-all-done.3 = f32[1,2,256,256]{3,1,0,2:T(2,128)S(1)} async-done(((f32[1,2,256,256]{3,1,0,2:T(2,128)}), f32[1,2,256,256]{3,1,0,2:T(2,128)S(1)}, u32[]{:S(2)}, u32[]{:S(2)}) %all-to-all-start.3) | async-done | bytes 524320 | tf_op jit(solution)/shard_map/all_to_all | solution.py:17
  87.2 1.9 %convolution_bitcast_fusion.3 = f32[128,512]{0,1:T(8,128)S(1)} fusion(f32[128,2,256]{0,2,1:T(8,128)S(1)} %get-tuple-element.25, f32[128,2,256]{0,2,1:T(8,128)S(1)} %get-tuple-element.27, f32[128,2,256]{0,2,1:T(8,128)S(1)} %get-tuple-element.26, f32[128,2,256]{0,2,1:T(8,128)S(1)} %get-tuple-element.24, f32[2,256,128]{1,2,0:T(8,128)S(1)} %copy.61, ...), kind=kOutput, calls=%fused_computation.15 | convolution fusion | flops 403701760 | bytes 1577984 | tf_op jit(solution)/shard_map/transpose(jvp(ikc,cf->fik))/dot_general | solution.py:30
  89.1 1.2 fusion.7
  90.3 0.8 copy-done.5
  91.2 1.0 copy.78
  92.2 4.9 %all-to-all-start.4 = ((f32[128,1,768]{2,1,0:T(1,128)}), f32[128,1,768]{2,1,0:T(1,128)S(1)}, u32[]{:S(2)}, u32[]{:S(2)}) async-start(f32[128,1,768]{2,1,0:T(1,128)} %copy.78), calls=%async_computation.4 | async-start | bytes 786432 | tf_op jit(solution)/shard_map/all_to_all | solution.py:112
  97.6 11.5 %all-to-all-done.4 = f32[128,1,768]{2,1,0:T(1,128)S(1)} async-done(((f32[128,1,768]{2,1,0:T(1,128)}), f32[128,1,768]{2,1,0:T(1,128)S(1)}, u32[]{:S(2)}, u32[]{:S(2)}) %all-to-all-start.4) | async-done | bytes 393248 | tf_op jit(solution)/shard_map/all_to_all | solution.py:112
  109.4 0.9 broadcast_in_dim.8
  110.4 4.8 %all-to-all-start.5 = ((f32[128,1,768]{2,1,0:T(1,128)}), f32[128,1,768]{2,1,0:T(1,128)S(1)}, u32[]{:S(2)}, u32[]{:S(2)}) async-start(f32[128,1,768]{2,1,0:T(1,128)} %broadcast_in_dim.8), calls=%async_computation.5 | async-start | bytes 786432 | tf_op jit(solution)/shard_map/all_to_all | solution.py:114
  115.3 0.8 copy.79
  116.1 11.1 %all-to-all-done.5 = f32[128,1,768]{2,1,0:T(1,128)S(1)} async-done(((f32[128,1,768]{2,1,0:T(1,128)}), f32[128,1,768]{2,1,0:T(1,128)S(1)}, u32[]{:S(2)}, u32[]{:S(2)}) %all-to-all-start.5) | async-done | bytes 393248 | tf_op jit(solution)/shard_map/all_to_all | solution.py:114
  127.9 0.7 slice.44
  (69 shorter events, 10.2 us)
Async XLA Ops:
  0.6 48.1 %copy-start = (f32[128,128]{1,0:T(8,128)S(1)}, f32[128,128]{1,0:T(8,128)}, u32[]{:S(2)}) copy-start(f32[128,128]{1,0:T(8,128)} %param.19) | copy-start | bytes 196612
  1.4 1.2 copy-start.2
  2.5 1.0 copy-start.3
  2.8 0.8 slice-start
  2.8 0.7 copy-start.7
  2.8 0.7 copy-start.10
  31.9 4.9 %copy-start.6 = (f32[640]{0:T(1024)S(1)}, f32[640]{0:T(1024)}, u32[]{:S(2)}) copy-start(f32[640]{0:T(1024)} %param.16) | copy-start | bytes 7684
  31.9 15.9 %all-to-all-start.1 = ((f32[1,1,256,256]{3,1,0,2:T(1,128)}), f32[1,1,256,256]{3,1,0,2:T(1,128)S(1)}, u32[]{:S(2)}, u32[]{:S(2)}) async-start(f32[1,1,256,256]{3,1,0,2:T(1,128)} %copy.66), calls=%async_computation.1 | async-start | bytes 524288 | tf_op jit(solution)/shard_map/all_to_all | solution.py:83
  48.6 1.0 copy-start.1
  48.7 0.8 copy-start.9
  68.0 4.5 %copy-start.12 = (f32[128]{0:T(128)S(1)}, f32[128]{0:T(128)}, u32[]{:S(2)}) copy-start(f32[128]{0:T(128)} %param.18) | copy-start | bytes 1540
  68.1 18.0 %all-to-all-start.3 = ((f32[1,2,256,256]{3,1,0,2:T(2,128)}), f32[1,2,256,256]{3,1,0,2:T(2,128)S(1)}, u32[]{:S(2)}, u32[]{:S(2)}) async-start(f32[1,2,256,256]{3,1,0,2:T(2,128)} %copy.70), calls=%async_computation.3 | async-start | bytes 1048576 | tf_op jit(solution)/shard_map/all_to_all | solution.py:17
  72.6 1.3 %copy-start.13 = (f32[128]{0:T(128)S(1)}, f32[128]{0:T(128)}, u32[]{:S(2)}) copy-start(f32[128]{0:T(128)} %param.20) | copy-start | bytes 1540
  86.5 0.7 copy-start.8
  86.5 0.7 copy-start.11
  87.2 1.9 %copy-start.4 = (f32[128,640]{1,0:T(8,128)S(1)}, f32[128,640]{1,0:T(8,128)}, u32[]{:S(2)}) copy-start(f32[128,640]{1,0:T(8,128)} %param.15) | copy-start | bytes 983044
  90.3 0.8 copy-start.5
  92.2 16.9 %all-to-all-start.4 = ((f32[128,1,768]{2,1,0:T(1,128)}), f32[128,1,768]{2,1,0:T(1,128)S(1)}, u32[]{:S(2)}, u32[]{:S(2)}) async-start(f32[128,1,768]{2,1,0:T(1,128)} %copy.78), calls=%async_computation.4 | async-start | bytes 786432 | tf_op jit(solution)/shard_map/all_to_all | solution.py:112
  110.4 16.9 %all-to-all-start.5 = ((f32[128,1,768]{2,1,0:T(1,128)}), f32[128,1,768]{2,1,0:T(1,128)S(1)}, u32[]{:S(2)}, u32[]{:S(2)}) async-start(f32[128,1,768]{2,1,0:T(1,128)} %broadcast_in_dim.8), calls=%async_computation.5 | async-start | bytes 786432 | tf_op jit(solution)/shard_map/all_to_all | solution.py:114
where the time goes:
time: 129 us
  waiting for transfers between devices  43 us (33%)
  blocking collectives  40 us (31%)
  starting transfers between devices  19.1 us (15%)
  local copies, waits for them, and re-layouts  12.2 us (9%)
  matrix products  10.4 us (8%)
  other arithmetic  2.76 us (2%)
    all_to_all x1, blocking collectives, side_by_side(): lax.all_to_all(both, axis, split_axis=split_dim, concat_axis=concat_dim,...  24.7 us
    all_to_all x1, blocking collectives, on_device(): lax.all_to_all(d_product.reshape(row_shape), ('row', 'ch'), split_axis=0,...  15.3 us
    all_to_all x1, waiting for transfers between devices, on_device(): lax.all_to_all(terms, ('row', 'ch'), split_axis=0, concat_axis=0, tiled=T...  11.5 us
    all_to_all x1, waiting for transfers between devices, on_device(): lax.all_to_all(jnp.broadcast_to(mine, terms.shape), ('row', 'ch'), split_...  11.1 us
    all_to_all x1, waiting for transfers between devices, on_device(): lax.all_to_all(product.reshape(per_device, 1, length, length), ('row', 'c...  10.3 us
    all_to_all x1, waiting for transfers between devices, side_by_side(): lax.all_to_all(both, axis, split_axis=split_dim, concat_axis=concat_dim,...  10.1 us
    unnamed x31, local copies, waits for them, and re-layouts  5 us
    all_to_all x1, starting transfers between devices, on_device(): lax.all_to_all(product.reshape(per_device, 1, length, length), ('row', 'c...  4.88 us
  transfers between devices with their start and end apart: 4, of which 4 were waited for; matrix products, arithmetic and copies ran while one was open for 4% of the time, Pallas kernels for 0%

commit v1 on v0

--- a/solution.py
+++ b/solution.py
@@ -80,12 +80,20 @@
     left_cols = left_cols.reshape(per_device, length, length)
     right_cols = right_cols.reshape(per_device, length, length)
     product = jnp.einsum("hik,hjk->hij", left_cols, right_cols, precision=lax.Precision.HIGHEST)
-    product_rows = lax.all_to_all(
-        product.reshape(per_device, 1, length, length),
-        ("row", "ch"),
-        split_axis=2,
-        concat_axis=0,
-        tiled=True,
+    product_rows = jnp.concatenate(
+        lax.all_to_all(
+            jnp.stack(
+                jnp.split(
+                    product.reshape(per_device, 1, length, length),
+                    lax.axis_size(("row", "ch")),
+                    axis=2,
+                )
+            ),
+            ("row", "ch"),
+            0,
+            0,
+        ),
+        axis=0,
     )
     product_rows = product_rows.reshape(hidden, row_count, length)
 

time: 129 us -> 202 us (1.57)
  local copies, waits for them, and re-layouts: 12.2 us -> 84.6 us
    unnamed x31 -> x156, local copies, waits for them, and re-layouts: 5 us -> 77.8 us
  transfers between devices with their start and end apart: 4 -> 4, of which waited for: 4 -> 4; matrix products, arithmetic and copies ran while one was open for 4% -> 2% of each run, Pallas kernels for 0% -> 0%
where the time goes in v1:
time: 202 us; the launch traced here: 201 us
  local copies, waits for them, and re-layouts  84.6 us (42%)
  waiting for transfers between devices  43.7 us (22%)
  blocking collectives  40.1 us (20%)
  starting transfers between devices  19.1 us (9%)
  matrix products  9.82 us (5%)
  other arithmetic  2.84 us (1%)
    unnamed x156, local copies, waits for them, and re-layouts  77.8 us
    all_to_all x1, blocking collectives, side_by_side(): lax.all_to_all(both, axis, split_axis=split_dim, concat_axis=concat_dim,...  24.7 us
    all_to_all x1, blocking collectives, on_device(): lax.all_to_all(d_product.reshape(row_shape), ('row', 'ch'), split_axis=0,...  15.3 us
    all_to_all x1, waiting for transfers between devices, on_device(): lax.all_to_all(terms, ('row', 'ch'), split_axis=0, concat_axis=0, tiled=T...  11.5 us
    all_to_all x1, waiting for transfers between devices, on_device(): lax.all_to_all(jnp.broadcast_to(mine, terms.shape), ('row', 'ch'), split_...  11.1 us
    all_to_all x1, waiting for transfers between devices, side_by_side(): lax.all_to_all(both, axis, split_axis=split_dim, concat_axis=concat_dim,...  10.8 us
    all_to_all x1, waiting for transfers between devices, on_device(): lax.all_to_all(jnp.stack(jnp.split(product.reshape(per_device, 1, length,...  10.3 us
    all_to_all x1, starting transfers between devices, on_device(): lax.all_to_all(jnp.stack(jnp.split(product.reshape(per_device, 1, length,...  4.88 us
  transfers between devices with their start and end apart: 4, of which 4 were waited for; matrix products, arithmetic and copies ran while one was open for 2% of the time, Pallas kernels for 0%

profile of v1, /device:TPU:1, one launch (start us, length us, event | category | flops | bytes accessed | tf_op | source)
XLA Modules:
  0.0 201.3 jit_solution(13742376978745176891)
XLA Ops:
  0.6 0.7 convert_element_type.3
  1.4 1.1 copy.4123
  2.8 0.7 copy-done.3
  3.5 1.1 fusion
  5.1 24.7 %all_to_all.68 = f32[128,2,2,256]{3,2,1,0:T(2,128)S(1)} all-to-all(f32[128,2,2,256]{3,2,1,0:T(2,128)S(1)} %copy.4126), channel_id=1, replica_groups=mesh['row'=32,'ch'=4] {'row','ch'}, dimensions={0} | all-to-all | bytes 1048576 | tf_op jit(solution)/shard_map/all_to_all | solution.py:17
  105.2 4.9 %all-to-all-start.1 = ((f32[128,1,1,2,256]{4,3,2,1,0:T(2,128)}), f32[128,1,1,2,256]{4,3,2,1,0:T(2,128)S(1)}, u32[]{:S(2)}, u32[]{:S(2)}) async-start(f32[128,1,1,2,256]{4,3,2,1,0:T(2,128)} %constant_dynamic-update-slice_fusion), calls=%async_computation.1 | async-start | bytes 524288 | tf_op jit(solution)/shard_map/all_to_all | solution.py:84
  110.8 10.3 %all-to-all-done.1 = f32[128,1,1,2,256]{4,3,2,1,0:T(2,128)S(1)} async-done(((f32[128,1,1,2,256]{4,3,2,1,0:T(2,128)}), f32[128,1,1,2,256]{4,3,2,1,0:T(2,128)S(1)}, u32[]{:S(2)}, u32[]{:S(2)}) %all-to-all-start.1) | async-done | bytes 262176 | tf_op jit(solution)/shard_map/all_to_all | solution.py:84
  121.4 0.8 copy-done.1
  123.7 15.3 %all_to_all.69 = f32[128,1,2,256]{3,2,1,0:T(2,128)S(1)} all-to-all(f32[128,1,2,256]{3,2,1,0:T(2,128)S(1)} %copy.4130), channel_id=1, replica_groups=mesh['row'=32,'ch'=4] {'row','ch'}, dimensions={0} | all-to-all | bytes 524288 | tf_op jit(solution)/shard_map/all_to_all | solution.py:105
  140.2 1.2 copy.4131
  141.4 4.5 %all-to-all-start.3 = ((f32[1,2,256,256]{3,1,0,2:T(2,128)}), f32[1,2,256,256]{3,1,0,2:T(2,128)S(1)}, u32[]{:S(2)}, u32[]{:S(2)}) async-start(f32[1,2,256,256]{3,1,0,2:T(2,128)} %copy.4131), calls=%async_computation.3 | async-start | bytes 1048576 | tf_op jit(solution)/shard_map/all_to_all | solution.py:17
  146.0 0.8 convolution_bitcast_fusion.4
  146.8 1.2 fusion.54
  148.6 10.8 %all-to-all-done.3 = f32[1,2,256,256]{3,1,0,2:T(2,128)S(1)} async-done(((f32[1,2,256,256]{3,1,0,2:T(2,128)}), f32[1,2,256,256]{3,1,0,2:T(2,128)S(1)}, u32[]{:S(2)}, u32[]{:S(2)}) %all-to-all-start.3) | async-done | bytes 524320 | tf_op jit(solution)/shard_map/all_to_all | solution.py:17
  160.6 1.9 convolution_bitcast_fusion.3
  162.5 1.2 fusion.7
  163.7 1.0 copy.4140
  164.8 4.9 %all-to-all-start.4 = ((f32[128,1,768]{2,1,0:T(1,128)}), f32[128,1,768]{2,1,0:T(1,128)S(1)}, u32[]{:S(2)}, u32[]{:S(2)}) async-start(f32[128,1,768]{2,1,0:T(1,128)} %copy.4140), calls=%async_computation.4 | async-start | bytes 786432 | tf_op jit(solution)/shard_map/all_to_all | solution.py:120
  170.2 11.5 %all-to-all-done.4 = f32[128,1,768]{2,1,0:T(1,128)S(1)} async-done(((f32[128,1,768]{2,1,0:T(1,128)}), f32[128,1,768]{2,1,0:T(1,128)S(1)}, u32[]{:S(2)}, u32[]{:S(2)}) %all-to-all-start.4) | async-done | bytes 393248 | tf_op jit(solution)/shard_map/all_to_all | solution.py:120
  182.0 0.9 broadcast_in_dim.8
  182.9 4.8 %all-to-all-start.5 = ((f32[128,1,768]{2,1,0:T(1,128)}), f32[128,1,768]{2,1,0:T(1,128)S(1)}, u32[]{:S(2)}, u32[]{:S(2)}) async-start(f32[128,1,768]{2,1,0:T(1,128)} %broadcast_in_dim.8), calls=%async_computation.5 | async-start | bytes 786432 | tf_op jit(solution)/shard_map/all_to_all | solution.py:122
  187.9 0.8 copy.4141
  188.7 11.1 %all-to-all-done.5 = f32[128,1,768]{2,1,0:T(1,128)S(1)} async-done(((f32[128,1,768]{2,1,0:T(1,128)}), f32[128,1,768]{2,1,0:T(1,128)S(1)}, u32[]{:S(2)}, u32[]{:S(2)}) %all-to-all-start.5) | async-done | bytes 393248 | tf_op jit(solution)/shard_map/all_to_all | solution.py:122
  200.5 0.7 slice.44
  (193 shorter events, 83.1 us)
Async XLA Ops:
  0.6 120.8 %copy-start = (f32[128,128]{1,0:T(8,128)S(1)}, f32[128,128]{1,0:T(8,128)}, u32[]{:S(2)}) copy-start(f32[128,128]{1,0:T(8,128)} %param.19) | copy-start | bytes 196612
  1.4 1.2 copy-start.2
  2.5 1.0 copy-start.3
  2.8 0.8 slice-start
  2.8 0.7 copy-start.6
  2.8 0.7 copy-start.9
  105.2 4.9 %copy-start.5 = (f32[640]{0:T(1024)S(1)}, f32[640]{0:T(1024)}, u32[]{:S(2)}) copy-start(f32[640]{0:T(1024)} %param.16) | copy-start | bytes 7684
  105.2 15.9 %all-to-all-start.1 = ((f32[128,1,1,2,256]{4,3,2,1,0:T(2,128)}), f32[128,1,1,2,256]{4,3,2,1,0:T(2,128)S(1)}, u32[]{:S(2)}, u32[]{:S(2)}) async-start(f32[128,1,1,2,256]{4,3,2,1,0:T(2,128)} %constant_dynamic-update-slice_fusion), calls=%async_computation.1 | async-start | bytes 524288 | tf_op jit(solution)/shard_map/all_to_all | solution.py:84
  121.2 1.0 copy-start.1
  121.2 0.9 copy-start.8
  141.4 4.5 %copy-start.11 = (f32[128]{0:T(128)S(1)}, f32[128]{0:T(128)}, u32[]{:S(2)}) copy-start(f32[128]{0:T(128)} %param.18) | copy-start | bytes 1540
  141.4 18.0 %all-to-all-start.3 = ((f32[1,2,256,256]{3,1,0,2:T(2,128)}), f32[1,2,256,256]{3,1,0,2:T(2,128)S(1)}, u32[]{:S(2)}, u32[]{:S(2)}) async-start(f32[1,2,256,256]{3,1,0,2:T(2,128)} %copy.4131), calls=%async_computation.3 | async-start | bytes 1048576 | tf_op jit(solution)/shard_map/all_to_all | solution.py:17
  146.0 0.8 copy-start.12
  159.9 0.7 copy-start.7
  159.9 0.7 copy-start.10
  160.6 1.9 copy-start.4
  164.8 16.9 %all-to-all-start.4 = ((f32[128,1,768]{2,1,0:T(1,128)}), f32[128,1,768]{2,1,0:T(1,128)S(1)}, u32[]{:S(2)}, u32[]{:S(2)}) async-start(f32[128,1,768]{2,1,0:T(1,128)} %copy.4140), calls=%async_computation.4 | async-start | bytes 786432 | tf_op jit(solution)/shard_map/all_to_all | solution.py:120
  182.9 16.9 %all-to-all-start.5 = ((f32[128,1,768]{2,1,0:T(1,128)}), f32[128,1,768]{2,1,0:T(1,128)S(1)}, u32[]{:S(2)}, u32[]{:S(2)}) async-start(f32[128,1,768]{2,1,0:T(1,128)} %broadcast_in_dim.8), calls=%async_computation.5 | async-start | bytes 786432 | tf_op jit(solution)/shard_map/all_to_all | solution.py:122
